TPU v7x, 32 devices: a whole 2x2x4 slice. The times are simulated.
32 devices in a mesh: expert: 2 (over y), blk: 16 (over z, x, core).
Axes of the slice: x: 2, y: 2, z: 4, core: 2. Of those that a mesh axis runs over, the one named last changes fastest.
Arguments:
- query_grads: bfloat16 [2, 16384, 2304], P('expert', 'blk'), may hold values from -0.125 to 0.125
- train_grads: bfloat16 [2, 128, 2304], P('expert', 'blk'), may hold values from -6 to 6
- counts: int32 [2, 128], P('expert', 'blk'), may hold values from 0 to 64
- factor: bfloat16 [2, 2304, 2304], P('expert', 'blk'), as said below
Outputs:
- scores: float32 [16384, 128], P('blk', 'expert')
Inputs may be any that keep to these rules, and one draw needn't show every extreme that they name: counts of tokens of one example, 0 where the expert gets none of them. Each expert's factor has the largest entry of each row on its diagonal.
All inputs are finite; a program needn't handle non-finite values.
Results may differ from a plain program's by a relative error of at most 0.0038.
Values may be sent and summed in bfloat16 or wider, within the bound.
A program may use at most 64 MiB of HBM per device.

v0:
```python
import functools

import jax
import jax.numpy as jnp
from jax import lax
from jax.experimental import pallas as pl
from jax.experimental.pallas import tpu as pltpu
from jax.sharding import PartitionSpec as P

TOKS_EX = 64
MESH = pl.DeviceIdType.MESH
NT = (((1,), (1,)), ((), ()))
CHUNKS = 4


def kernel(
    n_exp, n_chip,
    counts_ref, train_ref, query_hbm, factor_hbm, out_ref,
    query, factor, train_out, train_in, part, part_out, part_in, near_in,
    pre_out, pre_in, ker, kmat, score, score_out, score_in,
    query_sem, own_sem, pair_send, pair_recv,
    a_send, a_recv, b_send, b_recv, c_send, c_recv, d_send, d_recv,
    f_send, f_recv, e_send, e_recv,
):
    expert, blk = lax.axis_index("expert"), lax.axis_index("blk")
    chip, core = blk // 2, blk % 2
    mate = chip * 2 + (1 - core)
    peers = [lax.rem(chip + k, n_chip) for k in range(1, n_chip)]
    rivals = [lax.rem(expert + k, n_exp) for k in range(1, n_exp)]
    t_loc, depth = train_ref.shape[0], factor_hbm.shape[0]
    t_plane = t_loc * n_chip
    wide = 2 * depth

    own_copy = pltpu.make_async_copy(factor_hbm, factor.at[core], own_sem)
    own_copy.start()
    query_copy = pltpu.make_async_copy(query_hbm, query, query_sem)
    query_copy.start()

    barrier = pltpu.get_barrier_semaphore()
    for peer in peers:
        pl.semaphore_signal(barrier, inc=1, device_id=(expert, peer * 2 + core), device_id_type=MESH)
    pl.semaphore_signal(barrier, inc=1, device_id=(expert, mate), device_id_type=MESH)
    for rival in rivals:
        pl.semaphore_signal(barrier, inc=1, device_id=(rival, blk), device_id_type=MESH)

    train = train_ref[...].astype(jnp.float32)
    for c in range(n_chip):
        train_out[c] = train[:, c * wide:(c + 1) * wide].astype(jnp.bfloat16)
    pl.semaphore_wait(barrier, n_chip - 1 + 1 + n_exp - 1)

    def to_peers(source, target, send, recv):
        copies = []
        for k, peer in enumerate(peers):
            copy = pltpu.make_async_remote_copy(
                src_ref=source(peer), dst_ref=target(chip), send_sem=send.at[k],
                recv_sem=recv.at[chip], device_id=(expert, peer * 2 + core), device_id_type=MESH,
            )
            copy.start()
            copies.append(copy)
        return copies

    def from_peer(source, target, send, recv, k):
        peer = peers[k]
        pltpu.make_async_remote_copy(
            src_ref=source(peer), dst_ref=target(peer), send_sem=send.at[k],
            recv_sem=recv.at[peer], device_id=(expert, peer * 2 + core), device_id_type=MESH,
        ).wait_recv()

    a_args = (lambda c: train_out.at[c], lambda c: train_in.at[c], a_send, a_recv)
    a_copies = to_peers(*a_args)
    pair_copy = pltpu.make_async_remote_copy(
        src_ref=factor_hbm, dst_ref=factor.at[core], send_sem=pair_send, recv_sem=pair_recv,
        device_id=(expert, mate), device_id_type=MESH,
    )
    pair_copy.start()
    train_in[chip] = train_out[chip]
    own_copy.wait()
    pair_copy.wait_recv()
    for k in range(n_chip - 1):
        from_peer(*a_args, k)

    rows = train_in[...].astype(jnp.float32).reshape(t_plane, wide)
    first = rows[:, :depth].astype(jnp.bfloat16)
    second = rows[:, depth:].astype(jnp.bfloat16)
    share = jnp.dot(first, factor[0], preferred_element_type=jnp.float32)
    share = share + jnp.dot(second, factor[1], preferred_element_type=jnp.float32)
    share = share.reshape(n_chip, t_loc, share.shape[-1])
    part[...] = share
    part_out[...] = share.astype(jnp.bfloat16)
    half_chips = n_chip // 2
    base = chip // half_chips * half_chips
    near = [base + lax.rem(chip - base + k, half_chips) for k in range(1, half_chips)]
    far = [n_chip - half_chips - base + lax.rem(chip - base + k, half_chips) for k in range(half_chips)]
    order = [(peer, part_out, part_in) for peer in far] + [(peer, part, near_in) for peer in near]

    def share_copy(k, slot, peer, source, target):
        return pltpu.make_async_remote_copy(
            src_ref=source.at[peer], dst_ref=target.at[slot], send_sem=b_send.at[k],
            recv_sem=b_recv.at[slot], device_id=(expert, peer * 2 + core), device_id_type=MESH,
        )

    b_copies = [share_copy(k, chip, *entry) for k, entry in enumerate(order)]
    for copy in b_copies:
        copy.start()
    total = part[chip]
    for k, (peer, source, target) in reversed(list(enumerate(order))):
        share_copy(k, peer, peer, source, target).wait_recv()
        total = total + target[peer].astype(jnp.float32)
    at_row = lax.broadcasted_iota(jnp.int32, total.shape, 0)
    weight = jnp.zeros(total.shape, jnp.float32)
    for i in range(t_loc):
        weight = jnp.where(at_row == i, counts_ref[0, i].astype(jnp.float32) / TOKS_EX, weight)
    pre_out[...] = (total * weight).astype(jnp.bfloat16)

    c_args = (lambda c: pre_out, lambda c: pre_in.at[c], c_send, c_recv)
    c_copies = to_peers(*c_args)
    pre_in[chip] = pre_out[...]
    for k in range(n_chip - 1):
        from_peer(*c_args, k)
    pre = pre_in[...].astype(jnp.float32).reshape(t_plane, pre_in.shape[-1]).astype(jnp.bfloat16)
    halves = [
        lax.dot_general(factor[c], pre, NT, preferred_element_type=jnp.float32) for c in range(2)
    ]
    ker[core, chip] = jnp.concatenate(halves, axis=1).astype(jnp.bfloat16)

    d_args = (lambda c: ker.at[core, chip], lambda c: ker.at[core, c], d_send, d_recv)
    d_copies = to_peers(*d_args)
    f_copies = []

    def pass_on(c, k):
        copy = pltpu.make_async_remote_copy(
            src_ref=ker.at[core, c], dst_ref=ker.at[core, c], send_sem=f_send.at[k],
            recv_sem=f_recv.at[c], device_id=(expert, mate), device_id_type=MESH,
        )
        copy.start()
        f_copies.append(copy)

    pass_on(chip, n_chip - 1)
    for k in range(n_chip - 1):
        from_peer(*d_args, k)
        pass_on(peers[k], k)
    for c in range(n_chip):
        pltpu.make_async_remote_copy(
            src_ref=ker.at[1 - core, c], dst_ref=ker.at[1 - core, c], send_sem=f_send.at[c],
            recv_sem=f_recv.at[c], device_id=(expert, mate), device_id_type=MESH,
        ).wait_recv()

    t_all = 2 * t_plane
    for c in range(n_chip):
        even, odd = ker[0, c].astype(jnp.float32), ker[1, c].astype(jnp.float32)
        for half in range(2):
            cols = slice(half * t_plane, (half + 1) * t_plane)
            start = (2 * c + half) * depth
            both = jnp.concatenate([even[:, cols], odd[:, cols]], axis=1)
            kmat[start:start + depth, :] = both.astype(kmat.dtype)

    query_copy.wait()
    matrix = kmat[...].astype(jnp.bfloat16)
    step = query.shape[0] // CHUNKS
    t_out = t_all // n_exp
    e_copies = []
    for i in range(CHUNKS):
        found = jnp.dot(query[i * step:(i + 1) * step, :], matrix, preferred_element_type=jnp.float32).T
        pieces = []
        for c in range(n_chip):
            for plane in range(2):
                start = plane * t_plane + c * t_loc
                pieces.append(found[start:start + t_loc, :])
        ordered = jnp.concatenate(pieces, axis=0)
        for g in range(n_exp):
            block = ordered[g * t_out:(g + 1) * t_out, :]
            score[g, i] = block
            score_out[g, i] = block.astype(jnp.bfloat16)
        for k, rival in enumerate(rivals):
            copy = pltpu.make_async_remote_copy(
                src_ref=score_out.at[rival, i], dst_ref=score_in.at[expert, i],
                send_sem=e_send.at[k, i], recv_sem=e_recv.at[expert, i],
                device_id=(rival, blk), device_id_type=MESH,
            )
            copy.start()
            e_copies.append(copy)
    for i in range(CHUNKS):
        total = score[expert, i]
        for k, rival in enumerate(rivals):
            pltpu.make_async_remote_copy(
                src_ref=score_out.at[rival, i], dst_ref=score_in.at[rival, i],
                send_sem=e_send.at[k, i], recv_sem=e_recv.at[rival, i],
                device_id=(rival, blk), device_id_type=MESH,
            ).wait_recv()
            total = total + score_in[rival, i].astype(jnp.float32)
        out_ref[:, i * step:(i + 1) * step] = total
    pair_copy.wait_send()
    for copy in a_copies + b_copies + c_copies + d_copies + f_copies + e_copies:
        copy.wait_send()


def on_device(n_exp, n_blk, query_grads, train_grads, counts, factor):
    n_chip = n_blk // 2
    query_grads, train_grads, factor = query_grads[0], train_grads[0], factor[0]
    q_loc, width = query_grads.shape
    t_loc, depth = train_grads.shape[0], factor.shape[0]
    t_plane = t_loc * n_chip
    t_all = 2 * t_plane
    t_out = t_all // n_exp
    bf16, f32 = jnp.bfloat16, jnp.float32
    vmem = pl.BlockSpec(memory_space=pltpu.VMEM)
    hbm = pl.BlockSpec(memory_space=pl.ANY)
    dma = pltpu.SemaphoreType.DMA
    transposed = pl.pallas_call(
        functools.partial(kernel, n_exp, n_chip),
        out_shape=jax.ShapeDtypeStruct((t_out, q_loc), f32),
        in_specs=[pl.BlockSpec(memory_space=pltpu.SMEM), vmem, hbm, hbm],
        out_specs=vmem,
        scratch_shapes=[
            pltpu.VMEM((q_loc, width), bf16),
            pltpu.VMEM((2, depth, width), bf16),
            pltpu.VMEM((n_chip, t_loc, 2 * depth), bf16),
            pltpu.VMEM((n_chip, t_loc, 2 * depth), bf16),
            pltpu.VMEM((n_chip, t_loc, width), f32),
            pltpu.VMEM((n_chip, t_loc, width), bf16),
            pltpu.VMEM((n_chip, t_loc, width), bf16),
            pltpu.VMEM((n_chip, t_loc, width), f32),
            pltpu.VMEM((t_loc, width), bf16),
            pltpu.VMEM((n_chip, t_loc, width), bf16),
            pltpu.VMEM((2, n_chip, depth, 2 * t_plane), bf16),
            pltpu.VMEM((width, t_all), bf16 if depth % 16 == 0 else f32),
            pltpu.VMEM((n_exp, CHUNKS, t_out, q_loc // CHUNKS), f32),
            pltpu.VMEM((n_exp, CHUNKS, t_out, q_loc // CHUNKS), bf16),
            pltpu.VMEM((n_exp, CHUNKS, t_out, q_loc // CHUNKS), bf16),
            dma, dma, dma, dma,
            dma((n_chip,)), dma((n_chip,)), dma((n_chip,)), dma((n_chip,)),
            dma((n_chip,)), dma((n_chip,)), dma((n_chip,)), dma((n_chip,)),
            dma((n_chip,)), dma((n_chip,)), dma((n_exp, CHUNKS)), dma((n_exp, CHUNKS)),
        ],
        compiler_params=pltpu.CompilerParams(collective_id=0, has_side_effects=True),
        name="influence",
    )(counts, train_grads, query_grads, factor)
    return transposed.T


def solution(mesh):
    return jax.shard_map(
        functools.partial(on_device, mesh.shape["expert"], mesh.shape["blk"]),
        mesh=mesh,
        in_specs=(
            P("expert", "blk", None),
            P("expert", "blk", None),
            P("expert", "blk"),
            P("expert", "blk", None),
        ),
        out_specs=P("blk", "expert"),
        check_vma=False,
    )
```

profile of v0, /device:TPU:1, one launch (start us, length us, event | category | flops | bytes accessed | tf_op | source)
XLA Modules:
  0.0 41.5 jit_solution(14762427807593377989)
XLA Ops:
  0.0 39.9 %influence.1 = f32[64,1024]{1,0:T(8,128)} custom-call(s32[1,8]{1,0:T(1,128)} %counts_ref.1, bf16[8,2304]{1,0:T(8,128)(2,1)} %bitcast.7, bf16[1024,2304]{1,0:T(8,128)(2,1)} %bitcast.4, bf16[144,2304]{1,0:T(8,128)(2,1)} %bitcast.6), custom_call_target="tpu_custom_call" | custom-call | tf_op jit(solution)/shard_map/influence/pallas_call | solution.py:209
  39.9 1.7 %copy.6 = f32[1024,64]{0,1:T(8,128)} copy(f32[1024,64]{0,1:T(8,128)} %bitcast.5) | data formatting | bytes 524288
where the time goes:
time: 42 us; the launch traced here: 41.5 us
  Pallas kernels  39.9 us (95%)
  local copies, waits for them, and re-layouts  1.67 us (4%)
    pallas_call x1, Pallas kernels, on_device(): pl.pallas_call(functools.partial(kernel, n_exp, n_chip), out_shape=jax.Sh...  39.9 us
    unnamed x1, local copies, waits for them, and re-layouts  1.67 us

commit v1 on v0

v1 whole, which is shorter than its diff:
```python
import functools

import jax
import jax.numpy as jnp
from jax import lax
from jax.experimental import pallas as pl
from jax.experimental.pallas import tpu as pltpu
from jax.sharding import PartitionSpec as P

TOKS_EX = 64
MESH = pl.DeviceIdType.MESH
NT = (((1,), (1,)), ((), ()))
PIECES = 3
CHUNKS = 4


def kernel(
    n_exp, n_chip,
    counts_ref, train_ref, query_hbm, factor_hbm, out_ref,
    query, factor, train_out, train_in, part, part_out, part_in, near_in,
    pre_out, pre_in, ker, kmat, early, score, score_out, score_in,
    query_sem, own_sem, pair_send, pair_recv,
    a_send, a_recv, b_send, b_recv, c_send, c_recv, d_send, d_recv,
    f_send, f_recv, e_send, e_recv,
):
    expert, blk = lax.axis_index("expert"), lax.axis_index("blk")
    chip, core = blk // 2, blk % 2
    mate = chip * 2 + (1 - core)
    peers = [lax.rem(chip + k, n_chip) for k in range(1, n_chip)]
    rivals = [lax.rem(expert + k, n_exp) for k in range(1, n_exp)]
    t_loc, depth = train_ref.shape[0], factor_hbm.shape[0]
    width = factor_hbm.shape[1]
    t_plane = t_loc * n_chip
    wide = 2 * depth

    barrier = pltpu.get_barrier_semaphore()
    for peer in peers:
        pl.semaphore_signal(barrier, inc=1, device_id=(expert, peer * 2 + core), device_id_type=MESH)
    pl.semaphore_signal(barrier, inc=1, device_id=(expert, mate), device_id_type=MESH)
    for rival in rivals:
        pl.semaphore_signal(barrier, inc=1, device_id=(rival, blk), device_id_type=MESH)
    own_copy = pltpu.make_async_copy(factor_hbm, factor.at[core], own_sem)
    own_copy.start()
    query_copy = pltpu.make_async_copy(query_hbm, query, query_sem)
    query_copy.start()

    train = train_ref[...].astype(jnp.float32)
    for c in range(n_chip):
        train_out[c] = train[:, c * wide:(c + 1) * wide].astype(jnp.bfloat16)
    pl.semaphore_wait(barrier, n_chip - 1 + 1 + n_exp - 1)

    def to_peers(source, target, send, recv):
        copies = []
        for k, peer in enumerate(peers):
            copy = pltpu.make_async_remote_copy(
                src_ref=source(peer), dst_ref=target(chip), send_sem=send(k),
                recv_sem=recv(chip), device_id=(expert, peer * 2 + core), device_id_type=MESH,
            )
            copy.start()
            copies.append(copy)
        return copies

    def from_peer(source, target, send, recv, k):
        peer = peers[k]
        pltpu.make_async_remote_copy(
            src_ref=source(peer), dst_ref=target(peer), send_sem=send(k),
            recv_sem=recv(peer), device_id=(expert, peer * 2 + core), device_id_type=MESH,
        ).wait_recv()

    a_args = (lambda c: train_out.at[c], lambda c: train_in.at[c], lambda k: a_send.at[k], lambda c: a_recv.at[c])
    a_copies = to_peers(*a_args)
    pair_copy = pltpu.make_async_remote_copy(
        src_ref=factor_hbm, dst_ref=factor.at[core], send_sem=pair_send, recv_sem=pair_recv,
        device_id=(expert, mate), device_id_type=MESH,
    )
    pair_copy.start()
    train_in[chip] = train_out[chip]
    own_copy.wait()
    pair_copy.wait_recv()
    for k in range(n_chip - 1):
        from_peer(*a_args, k)

    rows = train_in[...].astype(jnp.float32).reshape(t_plane, wide)
    first = rows[:, :depth].astype(jnp.bfloat16)
    second = rows[:, depth:].astype(jnp.bfloat16)
    half_chips = n_chip // 2
    base = chip // half_chips * half_chips
    near = [base + lax.rem(chip - base + k, half_chips) for k in range(1, half_chips)]
    far = [n_chip - half_chips - base + lax.rem(chip - base + k, half_chips) for k in range(half_chips)]
    order = [(peer, part_out, part_in) for peer in far] + [(peer, part, near_in) for peer in near]
    span = width // PIECES
    pieces = [slice(s * span, (s + 1) * span) for s in range(PIECES)]

    def share_copy(k, s, slot, peer, source, target):
        return pltpu.make_async_remote_copy(
            src_ref=source.at[peer, :, pieces[s]], dst_ref=target.at[slot, :, pieces[s]], send_sem=b_send.at[k, s],
            recv_sem=b_recv.at[slot, s], device_id=(expert, peer * 2 + core), device_id_type=MESH,
        )

    b_copies = []
    for s, cols in enumerate(pieces):
        share = jnp.dot(first, factor[0, :, cols], preferred_element_type=jnp.float32)
        share = share + jnp.dot(second, factor[1, :, cols], preferred_element_type=jnp.float32)
        share = share.reshape(n_chip, t_loc, span)
        part[:, :, cols] = share
        part_out[:, :, cols] = share.astype(jnp.bfloat16)
        for k, entry in enumerate(order):
            copy = share_copy(k, s, chip, *entry)
            copy.start()
            b_copies.append(copy)

    at_row = lax.broadcasted_iota(jnp.int32, (t_loc, span), 0)
    weight = jnp.zeros((t_loc, span), jnp.float32)
    for i in range(t_loc):
        weight = jnp.where(at_row == i, counts_ref[0, i].astype(jnp.float32) / TOKS_EX, weight)

    def c_args(s):
        return (
            lambda c: pre_out.at[:, pieces[s]], lambda c: pre_in.at[c, :, pieces[s]],
            lambda k: c_send.at[k, s], lambda c: c_recv.at[c, s],
        )

    c_copies = []
    for s, cols in enumerate(pieces):
        total = part[chip, :, cols]
        for k, (peer, source, target) in reversed(list(enumerate(order))):
            share_copy(k, s, peer, peer, source, target).wait_recv()
            total = total + target[peer, :, cols].astype(jnp.float32)
        pre_out[:, cols] = (total * weight).astype(jnp.bfloat16)
        c_copies += to_peers(*c_args(s))
        pre_in[chip, :, cols] = pre_out[:, cols]

    halves = [None, None]
    for s, cols in enumerate(pieces):
        for k in range(n_chip - 1):
            from_peer(*c_args(s), k)
        pre = pre_in[:, :, cols].astype(jnp.float32).reshape(t_plane, span).astype(jnp.bfloat16)
        for c in range(2):
            more = lax.dot_general(factor[c, :, cols], pre, NT, preferred_element_type=jnp.float32)
            halves[c] = more if halves[c] is None else halves[c] + more
    ker[core, chip] = jnp.concatenate(halves, axis=1).astype(jnp.bfloat16)

    def d_copy(k, peer, slot):
        return pltpu.make_async_remote_copy(
            src_ref=ker.at[core, chip], dst_ref=ker.at[core, slot], send_sem=d_send.at[k],
            recv_sem=d_recv.at[slot], device_id=(expert, peer * 2 + core), device_id_type=MESH,
        )

    d_copies = [d_copy(k, peer, chip) for k, peer in enumerate(peers)]
    for copy in d_copies:
        copy.start()

    def pass_copy(c, plane):
        return pltpu.make_async_remote_copy(
            src_ref=ker.at[plane, c], dst_ref=ker.at[plane, c], send_sem=f_send.at[c],
            recv_sem=f_recv.at[c], device_id=(expert, mate), device_id_type=MESH,
        )

    pass_copy(chip, core).start()
    for copy in a_copies + b_copies + [pair_copy]:
        copy.wait_send()
    step = query.shape[0] // CHUNKS
    t_part = t_plane // n_exp
    half_width = width // 2
    e_copies = []

    def arrive(plane, group):
        @pl.when(core == plane)
        def own():
            for c in group:
                if c is not chip:
                    d_copy(0, c, c).wait_recv()
                    pass_copy(c, core).start()

        @pl.when(core != plane)
        def other():
            for c in group:
                pass_copy(c, 1 - core).wait_recv()

    def unpack(plane, j, h, group):
        first_chip = (chip // half_chips + h) % 2 * half_chips
        for k in range(half_chips):
            both = ker[plane, first_chip + k].astype(jnp.float32)
            for half in range(2):
                start = (2 * k + half) * depth
                rows = both[:, half * t_plane:(half + 1) * t_plane]
                kmat[j, h, start:start + depth, :] = rows.astype(kmat.dtype)

    def found(j, h, i):
        side = (chip // half_chips + h) % 2
        at = pl.ds(pl.multiple_of(side * half_width, half_width), half_width)
        return jnp.dot(
            query[i * step:(i + 1) * step, at], kmat[j, h].astype(jnp.bfloat16), preferred_element_type=jnp.float32
        )

    sides = ([chip] + near, far)
    for j, plane in enumerate((1, 0)):
        for h, group in enumerate(sides):
            arrive(plane, group)
            unpack(plane, j, h, group)
            if j == 0 and h == 0:
                query_copy.wait()
            for i in range(CHUNKS):
                if h == 0:
                    early[i] = found(j, h, i)
                    continue
                whole = (early[i] + found(j, h, i)).T
                for g in range(n_exp):
                    block = whole[g * t_part:(g + 1) * t_part, :]
                    score[j, g, i] = block
                    score_out[j, g, i] = block.astype(jnp.bfloat16)
                for k, rival in enumerate(rivals):
                    copy = pltpu.make_async_remote_copy(
                        src_ref=score_out.at[j, rival, i], dst_ref=score_in.at[j, expert, i],
                        send_sem=e_send.at[k, j, i], recv_sem=e_recv.at[expert, j, i],
                        device_id=(rival, blk), device_id_type=MESH,
                    )
                    copy.start()
                    e_copies.append(copy)
    for copy in c_copies + d_copies:
        copy.wait_send()
    for c in range(n_chip):
        pass_copy(c, core).wait_send()

    for j, plane in enumerate((1, 0)):
        for i in range(CHUNKS):
            total = score[j, expert, i]
            for k, rival in enumerate(rivals):
                pltpu.make_async_remote_copy(
                    src_ref=score_out.at[j, rival, i], dst_ref=score_in.at[j, rival, i],
                    send_sem=e_send.at[k, j, i], recv_sem=e_recv.at[rival, j, i],
                    device_id=(rival, blk), device_id_type=MESH,
                ).wait_recv()
                total = total + score_in[j, rival, i].astype(jnp.float32)
            for c in range(t_part // t_loc):
                at = (2 * c + plane) * t_loc
                out_ref[at:at + t_loc, i * step:(i + 1) * step] = total[c * t_loc:(c + 1) * t_loc, :]
    for copy in e_copies:
        copy.wait_send()


def on_device(n_exp, n_blk, query_grads, train_grads, counts, factor):
    n_chip = n_blk // 2
    query_grads, train_grads, factor = query_grads[0], train_grads[0], factor[0]
    q_loc, width = query_grads.shape
    t_loc, depth = train_grads.shape[0], factor.shape[0]
    t_plane = t_loc * n_chip
    t_part = t_plane // n_exp
    bf16, f32 = jnp.bfloat16, jnp.float32
    vmem = pl.BlockSpec(memory_space=pltpu.VMEM)
    hbm = pl.BlockSpec(memory_space=pl.ANY)
    dma = pltpu.SemaphoreType.DMA
    transposed = pl.pallas_call(
        functools.partial(kernel, n_exp, n_chip),
        out_shape=pltpu.VMEM((2 * t_part, q_loc), f32),
        in_specs=[pl.BlockSpec(memory_space=pltpu.SMEM), vmem, hbm, hbm],
        out_specs=vmem,
        scratch_shapes=[
            pltpu.VMEM((q_loc, width), bf16),
            pltpu.VMEM((2, depth, width), bf16),
            pltpu.VMEM((n_chip, t_loc, 2 * depth), bf16),
            pltpu.VMEM((n_chip, t_loc, 2 * depth), bf16),
            pltpu.VMEM((n_chip, t_loc, width), f32),
            pltpu.VMEM((n_chip, t_loc, width), bf16),
            pltpu.VMEM((n_chip, t_loc, width), bf16),
            pltpu.VMEM((n_chip, t_loc, width), f32),
            pltpu.VMEM((t_loc, width), bf16),
            pltpu.VMEM((n_chip, t_loc, width), bf16),
            pltpu.VMEM((2, n_chip, depth, 2 * t_plane), bf16),
            pltpu.VMEM((2, 2, width // 2, t_plane), bf16 if depth % 16 == 0 else f32),
            pltpu.VMEM((CHUNKS, q_loc // CHUNKS, t_plane), f32),
            pltpu.VMEM((2, n_exp, CHUNKS, t_part, q_loc // CHUNKS), f32),
            pltpu.VMEM((2, n_exp, CHUNKS, t_part, q_loc // CHUNKS), bf16),
            pltpu.VMEM((2, n_exp, CHUNKS, t_part, q_loc // CHUNKS), bf16),
            dma, dma, dma, dma,
            dma((n_chip,)), dma((n_chip,)), dma((n_chip, PIECES)), dma((n_chip, PIECES)),
            dma((n_chip, PIECES)), dma((n_chip, PIECES)), dma((n_chip,)), dma((n_chip,)),
            dma((n_chip,)), dma((n_chip,)), dma((n_exp, 2, CHUNKS)), dma((n_exp, 2, CHUNKS)),
        ],
        compiler_params=pltpu.CompilerParams(collective_id=0, has_side_effects=True),
        name="influence",
    )(counts, train_grads, query_grads, factor)
    return transposed.T


def solution(mesh):
    return jax.shard_map(
        functools.partial(on_device, mesh.shape["expert"], mesh.shape["blk"]),
        mesh=mesh,
        in_specs=(
            P("expert", "blk", None),
            P("expert", "blk", None),
            P("expert", "blk"),
            P("expert", "blk", None),
        ),
        out_specs=P("blk", "expert"),
        check_vma=False,
    )
```

time: 42 us -> 38.2 us (0.910)
  Pallas kernels: 39.9 us -> 37.1 us
  local copies, waits for them, and re-layouts: 1.67 us -> 0.71 us
    pallas_call x1, Pallas kernels: 39.9 us -> 37.1 us  [on_device(): pl.pallas_call(functools.partial(kernel, n_exp, n_chip), out_shape=pltpu....]
    unnamed x1, local copies, waits for them, and re-layouts: 1.67 us -> 0.71 us
where the time goes in v1:
time: 38.2 us; the launch traced here: 37.8 us
  Pallas kernels  37.1 us (97%)
  local copies, waits for them, and re-layouts  0.71 us (2%)
    pallas_call x1, Pallas kernels, on_device(): pl.pallas_call(functools.partial(kernel, n_exp, n_chip), out_shape=pltpu....  37.1 us

profile of v1, /device:TPU:1, one launch (start us, length us, event | category | flops | bytes accessed | tf_op | source)
XLA Modules:
  0.0 37.8 jit_solution(4940998127511161181)
XLA Ops:
  0.0 37.1 %influence.1 = f32[64,1024]{1,0:T(8,128)S(1)} custom-call(s32[1,8]{1,0:T(1,128)} %counts_ref.1, bf16[8,2304]{1,0:T(8,128)(2,1)} %bitcast.7, bf16[1024,2304]{1,0:T(8,128)(2,1)} %bitcast.5, bf16[144,2304]{1,0:T(8,128)(2,1)} %bitcast.6), custom_call_target="tpu_custom_call" | custom-call | tf_op jit(solution)/shard_map/influence/pallas_call | solution.py:253
  37.1 0.7 %copy.6 = f32[1024,64]{0,1:T(8,128)} copy(f32[1024,64]{0,1:T(8,128)S(1)} %bitcast.4) | data formatting | bytes 524288
